TPU v7x, 128 devices: a whole 4x4x4 slice. The times are simulated.
128 devices in a mesh: section: 2 (over core), dp: 16 (over y, x), tensor: 4 (over z).
Axes of the slice: x: 4, y: 4, z: 4, core: 2. Of those that a mesh axis runs over, the one named last changes fastest.
Arguments:
- layer_input: bfloat16 [2, 4096, 2, 4096], P('section', 'dp', None, 'tensor'), may hold values from -60 to 60
- norm_gain: float32 [2, 4096], P('section'), may hold values from 0.5 to 1.5
- upstream_grad: bfloat16 [2, 4096, 2, 4096], P('section', 'dp', None, 'tensor'), may hold values from -80 to 80
- saved_queries: bfloat16 [2, 4096, 2, 2048], P('section', 'dp', None, 'tensor'), may hold values from -150 to 150
- saved_keys: bfloat16 [2, 4096, 2, 1024], P('section', 'dp', None, 'tensor'), may hold values from -5 to 5
- saved_values: bfloat16 [2, 4096, 2, 1024], P('section', 'dp', None, 'tensor'), may hold values from -6 to 6
- segment_ids: int32 [2, 2, 4096], P('section', None, 'dp'), may hold values from 0 to 63, never falling along the last dimension, each value on 1 to 128 neighbouring positions
- batch_order: int32 [2, 16, 2], P('section', 'dp'), may hold values from 0 to 1, each once within a row
- qkv_weight: bfloat16 [2, 4096, 4096], P('section', None, 'tensor'), may hold values from -0.09375 to 0.09375
- out_weight: bfloat16 [2, 2048, 4096], P('section', 'tensor'), may hold values from -0.125 to 0.125
Outputs:
- passed_grad: bfloat16 [2, 4096, 2, 4096], P('section', 'dp', None, 'tensor')
- qkv_grad: float32 [2, 4096, 4096], P('section', 'dp', 'tensor')
- out_grad: float32 [2, 2048, 4096], P('section', 'tensor', 'dp')
- gain_grad: float32 [2, 4096], P('section', 'tensor')
All inputs are finite; a program needn't handle non-finite values.
Results may differ from a plain program's by a relative error of at most 0.0058.
The roundings to bfloat16 on the way count: a program that leaves them out, or rounds other values in their place, can miss the bound.
Values may be sent and summed in bfloat16 or wider, within the bound.
A program may use at most 192 MiB of HBM per device.

v0:
```python
import math
import jax
import jax.numpy as jnp
from jax import lax
from jax.sharding import PartitionSpec as P

HD = 128
KV = 8
HEADS = 16
EPS = 1e-05


def from_behind(value, axis, steps):
    count = lax.axis_size(axis)
    first, last = (max(0, -steps), min(count, count - steps))
    return lax.ppermute(value, axis, [(source, source + steps) for source in range(first, last)])


def attention_back(queries, saved_keys, saved_values, visible, attn_grad):
    score_scale = 1.0 / math.sqrt(HD)
    visible_full = visible[:, None, None, :, :]
    scores = (
        jnp.einsum("ibkgh,jbkh->bkgij", queries, saved_keys, preferred_element_type=jnp.float32)
        * score_scale
    )
    scores = jnp.where(visible_full, scores, -1e30)
    row_max = jnp.max(scores, axis=-1, keepdims=True)
    exp_scores = jnp.where(visible_full, jnp.exp(scores - row_max), 0.0)
    attn_probs = exp_scores / jnp.sum(exp_scores, axis=-1, keepdims=True)
    probs_bf16 = attn_probs.astype(jnp.bfloat16)
    attn_out = jnp.einsum(
        "bkgij,jbkh->ibkgh", probs_bf16, saved_values, preferred_element_type=jnp.float32
    ).astype(jnp.bfloat16)
    probs_grad = jnp.einsum(
        "ibkgh,jbkh->bkgij", attn_grad, saved_values, preferred_element_type=jnp.float32
    )
    row_dot = jnp.sum(attn_probs * probs_grad, axis=-1, keepdims=True)
    score_grad = (attn_probs * (probs_grad - row_dot) * score_scale).astype(jnp.bfloat16)
    query_grad = jnp.einsum(
        "bkgij,jbkh->ibkgh", score_grad, saved_keys, preferred_element_type=jnp.float32
    )
    key_grad = jnp.einsum(
        "bkgij,ibkgh->jbkh", score_grad, queries, preferred_element_type=jnp.float32
    )
    value_grad = jnp.einsum(
        "bkgij,ibkgh->jbkh", probs_bf16, attn_grad, preferred_element_type=jnp.float32
    )
    qkv_grads = jnp.concatenate(
        [query_grad, key_grad[..., None, :], value_grad[..., None, :]], axis=-2
    )
    return (attn_out, qkv_grads.astype(jnp.bfloat16))


def layer_back(
    inputs,
    upstream,
    queries,
    keys_local,
    values_local,
    segment_rows,
    gain_vec,
    weights_qkv,
    weights_out,
):
    seq_len, batch_count, local_width = inputs.shape
    inputs_full, upstream_full = (
        lax.all_gather(inputs, "tensor", axis=2, tiled=True),
        lax.all_gather(upstream, "tensor", axis=2, tiled=True),
    )
    model_width = inputs_full.shape[2]
    widened = inputs_full.astype(jnp.float32)
    root_mean = jnp.sqrt(jnp.mean(widened * widened, axis=-1, keepdims=True) + EPS)
    unit_rows = widened / root_mean
    normed_full = (unit_rows * gain_vec).astype(jnp.bfloat16)
    attn_grad = jnp.einsum(
        "ibd,cd->ibc", upstream_full, weights_out, preferred_element_type=jnp.float32
    ).astype(jnp.bfloat16)
    kv_local = keys_local.shape[-1] // HD
    group_size = HEADS // KV
    query_shape = (seq_len, batch_count, kv_local, group_size, HD)
    value_shape = (seq_len, batch_count, kv_local, HD)
    positions = jnp.arange(seq_len)
    causal = positions[None, :] <= positions[:, None]
    visible = (segment_rows[:, :, None] == segment_rows[:, None, :]) & causal[None]
    attn_out, qkv_grads = attention_back(
        queries.reshape(query_shape),
        keys_local.reshape(value_shape),
        values_local.reshape(value_shape),
        visible,
        attn_grad.reshape(query_shape),
    )
    attn_out = attn_out.reshape(seq_len, batch_count, -1)
    qkv_grads = qkv_grads.reshape(seq_len, batch_count, -1)
    grad_terms = jnp.einsum(
        "ibc,dc->ibd", qkv_grads, weights_qkv, preferred_element_type=jnp.float32
    )
    normed_grad = lax.psum_scatter(grad_terms, "tensor", scatter_dimension=2, tiled=True)
    first_col = lax.axis_index("tensor") * local_width
    unit_local = lax.dynamic_slice_in_dim(unit_rows, first_col, local_width, 2)
    gain_local = lax.dynamic_slice_in_dim(gain_vec, first_col, local_width, 0)
    scaled = normed_grad * gain_local
    row_part = jnp.sum(scaled * unit_local, axis=-1, keepdims=True)
    row_total = lax.psum(row_part, "tensor")
    through = (
        upstream.astype(jnp.float32) + (scaled - unit_local * (row_total / model_width)) / root_mean
    )
    gain_part = jnp.sum(normed_grad * unit_local, axis=(0, 1))
    return (
        through.astype(jnp.bfloat16),
        gain_part,
        normed_full,
        upstream_full,
        attn_out,
        qkv_grads,
    )


def shards(
    layer_input,
    norm_gain,
    upstream_grad,
    saved_queries,
    saved_keys,
    saved_values,
    segment_ids,
    batch_order,
    qkv_weight,
    out_weight,
):
    inputs = layer_input[0]
    upstream = upstream_grad[0]
    gain_vec = norm_gain[0]
    queries = saved_queries[0]
    keys_local = saved_keys[0]
    values_local = saved_values[0]
    id_rows = segment_ids[0]
    order_row = batch_order[0, 0]
    weights_qkv = qkv_weight[0]
    weights_out = out_weight[0]
    through, gain_part, normed_full, upstream_full, attn_out, qkv_grads = layer_back(
        inputs,
        upstream,
        queries,
        keys_local,
        values_local,
        id_rows,
        gain_vec,
        weights_qkv,
        weights_out,
    )
    ordered = jnp.take(through, order_row, axis=1)
    passed = from_behind(ordered, "section", -1)
    replicas = lax.axis_size("dp")
    qkv_total = jnp.einsum(
        "ibd,ibc->dc", normed_full, qkv_grads, preferred_element_type=jnp.float32
    )
    out_total = jnp.einsum(
        "ibc,ibd->cd", attn_out, upstream_full, preferred_element_type=jnp.float32
    )
    qkv_grad = lax.psum_scatter(qkv_total, "dp", scatter_dimension=0, tiled=True) / replicas
    out_grad = lax.psum_scatter(out_total, "dp", scatter_dimension=1, tiled=True) / replicas
    gain_grad = lax.psum(gain_part, "dp") / replicas
    return (passed[None], qkv_grad[None], out_grad[None], gain_grad[None])


def solution(mesh):
    placed = (
        P("section", "dp", None, "tensor"),
        P("section", None),
        P("section", "dp", None, "tensor"),
        P("section", "dp", None, "tensor"),
        P("section", "dp", None, "tensor"),
        P("section", "dp", None, "tensor"),
        P("section", None, "dp"),
        P("section", "dp", None),
        P("section", None, "tensor"),
        P("section", "tensor", None),
    )
    return jax.shard_map(
        shards,
        mesh=mesh,
        in_specs=placed,
        out_specs=(
            P("section", "dp", None, "tensor"),
            P("section", "dp", "tensor"),
            P("section", "tensor", "dp"),
            P("section", "tensor"),
        ),
        check_vma=False,
    )
```

profile of v0, /device:TPU:1, one launch (start us, length us, event | category | flops | bytes accessed | tf_op | source)
XLA Modules:
  0.0 406.7 jit_solution(5581653968323635845)
XLA Ops:
  7.2 0.0 copy-start.3
  7.2 0.0 all-gather.5.cloned.1.call-start
  7.2 2.5 copy.14
  9.8 0.0 all-gather.5.cloned.1.call-update
  9.8 0.0 copy-start.6
  9.8 0.0 all-gather.7.cloned.1.call-start
  9.9 0.0 copy-done.3
  9.9 1.2 copy.27
  11.1 0.0 all-gather.7.cloned.1.call-update
  11.1 0.0 reduce-scatter.4.cloned.1.call-start
  11.2 0.0 copy-done.5
  11.2 0.2 reshape_squeeze.9
  11.4 0.2 copy.36
  11.5 0.0 copy-done.6
  11.6 0.0 copy-start.7
  11.6 0.2 reshape_squeeze.11
  11.7 0.2 copy.45
  11.9 0.2 copy-done.4
  12.2 0.5 copy.54
  12.7 0.0 copy-done.9
  12.7 0.2 compare_and_fusion
  12.9 2.4 fusion.35
  15.3 0.0 copy-done.7
  15.3 46.4 %all-gather.5.cloned.1.call-done = bf16[1,256,2,4096]{3,1,2,0:T(8,128)(2,1)} async-done(((bf16[1,256,2,1024]{3,1,2,0:T(8,128)(2,1)}), bf16[1,256,2,4096]{3,1,2,0:T(8,128)(2,1)}) %all-gather.5.cloned.1.call-update) | async-done | bytes 4194320 | tf_op jit(solution)/shard_map/all_gather | solution.py:68
  61.7 5.8 %fusion.15 = bf16[256,2,512]{2,0,1:T(8,128)(2,1)S(1)} fusion(bf16[1,512,4096]{2,1,0:T(8,128)(2,1)} %param.19, bf16[1,256,2,4096]{3,1,2,0:T(8,128)(2,1)} %all-gather.5.cloned.1.call-done), kind=kOutput, calls=%fused_computation.30 | convolution fusion | flops 2147745792 | bytes 8912896 | tf_op jit(solution)/shard_map/ibd,cd->ibc/dot_general | solution.py:75
  67.5 0.2 copy.55
  67.7 0.5 fusion.36
  68.2 3.7 convolution_bitcast_fusion.4
  71.9 3.5 convolution_bitcast_fusion.2
  75.4 0.0 copy-start.8
  75.4 2.3 convolution_bitcast_fusion.3
  77.7 0.1 maximum_convert_fusion
  77.8 10.3 %fusion.3 = f32[256,2,4096]{2,0,1:T(8,128)} fusion(bf16[256,2,1024]{0,2,1:T(8,128)(2,1)S(1)} %bitcast.116, bf16[1,4096,1024]{2,1,0:T(8,128)(2,1)} %param.18), kind=kOutput, calls=%fused_computation.7 | convolution fusion | flops 4294967296 | bytes 17825792 | tf_op jit(solution)/shard_map/ibc,dc->ibd/dot_general | solution.py:94
  88.1 0.0 reduce-scatter.4.cloned.1.call-update
  88.1 0.2 reduce-scatter.8.cloned.1.call-start
  88.4 0.0 copy-start.2
  88.4 2.1 convolution_convert_fusion
  90.5 0.8 copy-done.2
  91.2 5.6 %convolution_bitcast_fusion.1 = f32[512,4096]{1,0:T(8,128)} fusion(bf16[256,2,512]{0,2,1:T(8,128)(2,1)S(1)} %bitcast.121, bf16[1,256,2,4096]{3,1,2,0:T(8,128)(2,1)S(1)} %copy-done.2), kind=kOutput, calls=%fused_computation.10 | convolution fusion | flops 2147483648 | bytes 13107200 | tf_op jit(solution)/shard_map/ibc,ibd->cd/dot_general | solution.py:157
  96.8 0.0 reduce-scatter.8.cloned.1.call-update
  96.8 0.0 reduce-scatter.6.cloned.1.call-start
  96.9 15.8 %all-gather.7.cloned.1.call-done = bf16[1,256,2,4096]{3,1,2,0:T(8,128)(2,1)} async-done(((bf16[1,256,2,1024]{3,1,2,0:T(8,128)(2,1)}), bf16[1,256,2,4096]{3,1,2,0:T(8,128)(2,1)}) %all-gather.7.cloned.1.call-update) | async-done | bytes 4194320 | tf_op jit(solution)/shard_map/all_gather | solution.py:67
  112.7 3.2 fusion.2
  115.9 0.2 copy-done
  116.1 8.5 %convolution_bitcast_fusion = f32[4096,1024]{1,0:T(8,128)} fusion(bf16[256,2,1024]{0,2,1:T(8,128)(2,1)S(1)} %bitcast.117, f32[4096]{0:T(1024)S(1)} %bitcast.129, bf16[1,256,2,4096]{3,1,2,0:T(8,128)(2,1)S(1)} %copy-done, f32[256,2]{0,1:T(2,128)S(1)} %add_sqrt_fusion), kind=kOutput, calls=%fused_computation.5 | convolution fusion | flops 4303355904 | bytes 22038528 | tf_op jit(solution)/shard_map/ibd,ibc->dc/dot_general | solution.py:154
  124.7 0.0 reduce-scatter.6.cloned.1.call-update
  124.7 0.6 copy-done.11
  125.4 6.7 %convert_divide_fusion = f32[256,2,4096]{2,0,1:T(8,128)} fusion(bf16[1,256,2,4096]{3,1,2,0:T(8,128)(2,1)} %all-gather.7.cloned.1.call-done, f32[256,2]{0,1:T(2,128)S(1)} %add_sqrt_fusion), kind=kLoop, calls=%fused_computation.3 | loop fusion | flops 4194304 | bytes 12584960 | tf_op jit(solution)/shard_map/div | solution.py:73
  132.1 64.0 %reduce-scatter.4.cloned.1.call-done = f32[256,2,1024]{2,0,1:T(8,128)} async-done(((f32[256,2,4096]{2,0,1:T(8,128)}), f32[256,2,1024]{2,0,1:T(8,128)}) %reduce-scatter.4.cloned.1.call-update) | async-done | bytes 2097168 | tf_op jit(solution)/shard_map/reduce_scatter | solution.py:97
  196.1 2.9 multiply_reduce_fusion
  199.0 6.5 %psum.14 = f32[256,2,1]{0,1,2:T(2,128)S(1)} all-reduce(f32[256,2,1]{0,1,2:T(2,128)S(1)} %bitcast.126), channel_id=1, replica_groups=mesh['section'=2,'dp'=16,'tensor'=4] {'tensor'}, use_global_device_ids=true, to_apply=%region_6.7 | all-reduce | flops 512 | bytes 4096 | tf_op jit(solution)/shard_map/psum | solution.py:103
  205.5 0.0 copy-done.1
  205.5 2.3 fusion.10
  207.9 0.6 gather_fusion
  208.5 0.2 select_bitcast_fusion
  208.7 5.1 %collective-permute-start = (bf16[256,2,1024]{2,0,1:T(8,128)(2,1)S(1)}, bf16[256,2,1024]{2,0,1:T(8,128)(2,1)S(1)}, u32[]{:S(2)}, u32[]{:S(2)}) collective-permute-start(bf16[256,2,1024]{2,0,1:T(8,128)(2,1)S(1)} %select_bitcast_fusion), channel_id=1, source_target_pairs={{64,0},{65,1},{66,2},{67,3},{68,4},{69,5},{70,6},{71,7},{72,8},{73... | collective-permute-start | bytes 3145736 | tf_op jit(solution)/shard_map/ppermute | solution.py:16
  213.7 33.7 %psum.15 = f32[1024]{0:T(1024)S(1)} all-reduce(f32[1024]{0:T(1024)S(1)} %get-tuple-element.8), channel_id=1, replica_groups=mesh['section'=2,'dp'=16,'tensor'=4] {'dp'}, use_global_device_ids=true, to_apply=%region_10.11 | all-reduce | flops 1024 | bytes 8192 | tf_op jit(solution)/shard_map/psum | solution.py:162
  247.4 0.6 broadcast_multiply_fusion
  248.0 35.4 %reduce-scatter.8.cloned.1.call-done = f32[512,256]{1,0:T(8,128)} async-done(((f32[512,4096]{1,0:T(8,128)}), f32[512,256]{1,0:T(8,128)}) %reduce-scatter.8.cloned.1.call-update) | async-done | bytes 524304 | tf_op jit(solution)/shard_map/reduce_scatter | solution.py:161
  283.4 1.9 multiply_bitcast_fusion.1
  285.3 0.0 collective-permute-done
  285.3 2.0 copy.32
  287.3 110.5 %reduce-scatter.6.cloned.1.call-done = f32[256,1024]{1,0:T(8,128)} async-done(((f32[4096,1024]{1,0:T(8,128)}), f32[256,1024]{1,0:T(8,128)}) %reduce-scatter.6.cloned.1.call-update) | async-done | bytes 1048592 | tf_op jit(solution)/shard_map/reduce_scatter | solution.py:160
  397.8 2.3 multiply_bitcast_fusion
  (16 shorter events, 0.1 us)
Async XLA Ops:
  7.2 2.7 copy-start.3
  7.2 54.5 %all-gather.5.cloned.1.call-start = ((), (), s32[]{:S(2)}) async-start(), calls=%async_computation.6 | async-start | bytes 5242880 | tf_op jit(solution)/shard_map/all_gather | solution.py:68
  9.8 1.4 copy-start.5
  9.8 1.8 copy-start.6
  9.8 102.9 %all-gather.7.cloned.1.call-start = ((), (), s32[]{:S(2)}) async-start(), calls=%async_computation.7 | async-start | bytes 5242880 | tf_op jit(solution)/shard_map/all_gather | solution.py:67
  11.1 1.0 copy-start.4
  11.1 1.6 copy-start.9
  11.1 185.0 %reduce-scatter.4.cloned.1.call-start = ((), (), s32[]{:S(2)}) async-start(), calls=%async_computation.3 | async-start | bytes 10485760 | tf_op jit(solution)/shard_map/reduce_scatter | solution.py:97
  11.6 3.7 copy-start.7
  75.4 2.3 copy-start.8
  88.1 195.3 %reduce-scatter.8.cloned.1.call-start = ((), (), s32[]{:S(2)}) async-start(), calls=%async_computation.5 | async-start | bytes 8912896 | tf_op jit(solution)/shard_map/reduce_scatter | solution.py:161
  88.4 2.9 copy-start.2
  96.8 19.1 %copy-start.10 = (f32[1,4096]{1,0:T(1,128)S(1)}, f32[1,4096]{1,0:T(1,128)}, u32[]{:S(2)}) copy-start(f32[1,4096]{1,0:T(1,128)} %param.11) | copy-start | bytes 49156
  96.8 301.0 %reduce-scatter.6.cloned.1.call-start = ((), (), s32[]{:S(2)}) async-start(), calls=%async_computation.4 | async-start | bytes 17825792 | tf_op jit(solution)/shard_map/reduce_scatter | solution.py:160
  112.7 3.4 copy-start
  124.7 0.7 copy-start.11
  196.1 9.4 %copy-start.1 = (f32[256,2,1024]{2,0,1:T(8,128)S(1)}, f32[256,2,1024]{2,0,1:T(8,128)}, u32[]{:S(2)}) copy-start(f32[256,2,1024]{2,0,1:T(8,128)} %reduce-scatter.4.cloned.1.call-done) | copy-start | bytes 6291460
  208.7 76.6 %collective-permute-start = (bf16[256,2,1024]{2,0,1:T(8,128)(2,1)S(1)}, bf16[256,2,1024]{2,0,1:T(8,128)(2,1)S(1)}, u32[]{:S(2)}, u32[]{:S(2)}) collective-permute-start(bf16[256,2,1024]{2,0,1:T(8,128)(2,1)S(1)} %select_bitcast_fusion), channel_id=1, source_target_pairs={{64,0},{65,1},{66,2},{67,3},{68,4},{69,5},{70,6},{71,7},{72,8},{73... | collective-permute-start | bytes 3145736 | tf_op jit(solution)/shard_map/ppermute | solution.py:16
Sparse Core Ops, SparseCore 0:
  10.2 51.4 all-gather.4
  63.9 48.6 all-gather.6
  115.2 80.9 reduce-scatter.3
  199.4 83.9 reduce-scatter.7
  286.7 111.1 reduce-scatter.5
where the time goes:
time: 407 us
  waiting for transfers between devices  272 us (67%)
  matrix products  44.6 us (11%)
  blocking collectives  40.2 us (10%)
  other arithmetic  20.5 us (5%)
  between operations  14 us (3%)
  local copies, waits for them, and re-layouts  9.74 us (2%)
  starting transfers between devices  5.44 us (1%)
    reduce_scatter x1, waiting for transfers between devices, shards(): lax.psum_scatter(qkv_total, 'dp', scatter_dimension=0, tiled=True)  110 us
    reduce_scatter x1, waiting for transfers between devices, layer_back(): lax.psum_scatter(grad_terms, 'tensor', scatter_dimension=2, tiled=True)  64 us
    all_gather x1, waiting for transfers between devices, layer_back(): lax.all_gather(upstream, 'tensor', axis=2, tiled=True)  46.4 us
    reduce_scatter x1, waiting for transfers between devices, shards(): lax.psum_scatter(out_total, 'dp', scatter_dimension=1, tiled=True)  35.4 us
    psum x1, blocking collectives, shards(): gain_grad = lax.psum(gain_part, 'dp') / replicas  33.7 us
    all_gather x1, waiting for transfers between devices, layer_back(): lax.all_gather(inputs, 'tensor', axis=2, tiled=True)  15.8 us
    dot_general x1, matrix products, layer_back(): jnp.einsum('ibc,dc->ibd', qkv_grads, weights_qkv, preferred_element_type=...  10.3 us
    dot_general x1, matrix products, shards(): jnp.einsum('ibd,ibc->dc', normed_full, qkv_grads, preferred_element_type=...  8.55 us
  transfers between devices with their start and end apart: 6, of which 5 were waited for; matrix products, arithmetic and copies ran while one was open for 17% of the time, Pallas kernels for 0%

commit v1 on v0

--- a/solution.py
+++ b/solution.py
@@ -1,3 +1,4 @@
+import functools
 import math
 import jax
 import jax.numpy as jnp
@@ -8,6 +9,18 @@
 KV = 8
 HEADS = 16
 EPS = 1e-05
+
+
+def divide_the_files(vec, device_axis):
+    history = []
+    for _ in range(lax.axis_size(device_axis)):
+        history.append(vec)
+    q_next = jnp.stack(history)
+    top = jnp.concatenate(lax.all_to_all(q_next, device_axis, 0, 0), 2)
+    return top
+
+
+apply_seats_all_now = functools.partial(divide_the_files, device_axis="tensor")
 
 
 def from_behind(value, axis, steps):
@@ -64,7 +77,7 @@
 ):
     seq_len, batch_count, local_width = inputs.shape
     inputs_full, upstream_full = (
-        lax.all_gather(inputs, "tensor", axis=2, tiled=True),
+        apply_seats_all_now(inputs),
         lax.all_gather(upstream, "tensor", axis=2, tiled=True),
     )
     model_width = inputs_full.shape[2]

time: 407 us -> 426 us (1.047)
  blocking collectives: 40.2 us -> 136 us
  waiting for transfers between devices: 272 us -> 196 us
  local copies, waits for them, and re-layouts: 9.74 us -> 16.2 us
  other arithmetic: 20.5 us -> 15.1 us
    all_to_all x0 -> x1, blocking collectives: none -> 96 us  [divide_the_files(): top = jnp.concatenate(lax.all_to_all(q_next, device_axis, 0, 0), 2)]
    reduce_scatter x1, waiting for transfers between devices: 64 us -> 2.16 us  [layer_back(): lax.psum_scatter(grad_terms, 'tensor', scatter_dimension=2, tiled=True)]
    all_gather x1 -> x0, waiting for transfers between devices: 15.8 us -> none  [layer_back(): lax.all_gather(inputs, 'tensor', axis=2, tiled=True)]
    div x1, other arithmetic: 6.71 us -> 1.48 us  [layer_back(): unit_rows = widened / root_mean]
    unnamed x27 -> x26, local copies, waits for them, and re-layouts: 7.72 us -> 11.7 us
  transfers between devices with their start and end apart: 6 -> 5, of which waited for: 5 -> 4; matrix products, arithmetic and copies ran while one was open for 17% -> 8% of each run, Pallas kernels for 0% -> 0%
where the time goes in v1:
time: 426 us
  waiting for transfers between devices  196 us (46%)
  blocking collectives  136 us (32%)
  matrix products  43 us (10%)
  local copies, waits for them, and re-layouts  16.2 us (4%)
  other arithmetic  15.1 us (4%)
  between operations  14 us (3%)
  starting transfers between devices  5.43 us (1%)
    reduce_scatter x1, waiting for transfers between devices, shards(): lax.psum_scatter(qkv_total, 'dp', scatter_dimension=0, tiled=True)  111 us
    all_to_all x1, blocking collectives, divide_the_files(): top = jnp.concatenate(lax.all_to_all(q_next, device_axis, 0, 0), 2)  96 us
    all_gather x1, waiting for transfers between devices, layer_back(): lax.all_gather(upstream, 'tensor', axis=2, tiled=True)  47.8 us
    reduce_scatter x1, waiting for transfers between devices, shards(): lax.psum_scatter(out_total, 'dp', scatter_dimension=1, tiled=True)  35.6 us
    psum x1, blocking collectives, shards(): gain_grad = lax.psum(gain_part, 'dp') / replicas  33.7 us
    unnamed x26, local copies, waits for them, and re-layouts  11.7 us
    dot_general x1, matrix products, layer_back(): jnp.einsum('ibc,dc->ibd', qkv_grads, weights_qkv, preferred_element_type=...  10.3 us
  transfers between devices with their start and end apart: 5, of which 4 were waited for; matrix products, arithmetic and copies ran while one was open for 8% of the time, Pallas kernels for 0%

profile of v1, /device:TPU:1, one launch (start us, length us, event | category | flops | bytes accessed | tf_op | source)
XLA Modules:
  0.0 426.0 jit_solution(5343442801518033539)
XLA Ops:
  7.2 0.0 copy-start.6
  7.2 0.0 copy-start.7
  7.2 0.0 all-gather.3.cloned.1.call-start
  7.2 2.5 copy.33
  9.8 0.0 all-gather.3.cloned.1.call-update
  9.8 0.0 reduce-scatter.4.cloned.1.call-start
  9.8 0.0 copy-done.6
  9.8 0.2 reshape_squeeze.9
  10.0 0.2 copy.56
  10.2 0.0 copy-done.7
  10.2 0.2 reshape_squeeze.11
  10.4 0.2 copy.65
  10.5 0.3 copy-done.4
  10.8 0.5 copy.74
  11.3 0.0 copy-start.5
  11.4 0.0 copy-done.9
  11.4 0.2 compare_and_fusion
  11.6 2.4 fusion.35
  13.9 0.0 copy-done.5
  13.9 47.8 %all-gather.3.cloned.1.call-done = bf16[1,256,2,4096]{3,1,2,0:T(8,128)(2,1)} async-done(((bf16[1,256,2,1024]{3,1,2,0:T(8,128)(2,1)}), bf16[1,256,2,4096]{3,1,2,0:T(8,128)(2,1)}) %all-gather.3.cloned.1.call-update) | async-done | bytes 4194320 | tf_op jit(solution)/shard_map/all_gather | solution.py:81
  61.7 5.8 %fusion.15 = bf16[256,2,512]{2,0,1:T(8,128)(2,1)S(1)} fusion(bf16[1,512,4096]{2,1,0:T(8,128)(2,1)} %param.19, bf16[1,256,2,4096]{3,1,2,0:T(8,128)(2,1)} %all-gather.3.cloned.1.call-done), kind=kOutput, calls=%fused_computation.31 | convolution fusion | flops 2147745792 | bytes 8912896 | tf_op jit(solution)/shard_map/ibd,cd->ibc/dot_general | solution.py:88
  67.5 0.2 copy.75
  67.8 0.5 fusion.36
  68.2 1.1 copy-done.11
  69.3 0.5 convolution_bitcast_fusion.3
  69.8 3.8 convolution_bitcast_fusion.4
  73.6 3.8 convolution_bitcast_fusion.2
  77.5 1.2 maximum_convert_fusion
  78.7 10.3 %fusion.3 = f32[256,2,4096]{2,0,1:T(8,128)} fusion(bf16[256,2,1024]{0,2,1:T(8,128)(2,1)S(1)} %bitcast.113, bf16[1,4096,1024]{2,1,0:T(8,128)(2,1)} %param.18), kind=kOutput, calls=%fused_computation.7 | convolution fusion | flops 4294967296 | bytes 17825792 | tf_op jit(solution)/shard_map/ibc,dc->ibd/dot_general | solution.py:107
  89.0 0.0 reduce-scatter.4.cloned.1.call-update
  89.1 0.0 reduce-scatter.8.cloned.1.call-start
  89.1 2.1 convolution_convert_fusion
  91.2 0.7 copy-done.2
  91.9 5.6 %convolution_bitcast_fusion.1 = f32[512,4096]{1,0:T(8,128)} fusion(bf16[256,2,512]{0,2,1:T(8,128)(2,1)S(1)} %bitcast.121, bf16[1,256,2,4096]{3,1,2,0:T(8,128)(2,1)S(1)} %copy-done.2), kind=kOutput, calls=%fused_computation.10 | convolution fusion | flops 2147483648 | bytes 13107200 | tf_op jit(solution)/shard_map/ibc,ibd->cd/dot_general | solution.py:170
  97.5 0.0 reduce-scatter.8.cloned.1.call-update
  97.5 0.2 reduce-scatter.6.cloned.1.call-start
  97.7 1.2 copy-done.3
  98.9 0.3 copy.46
  99.2 0.5 stack.3
  99.7 96.0 %all_to_all.5 = bf16[4,256,2,1024]{3,1,2,0:T(8,128)(2,1)S(1)} all-to-all(bf16[4,256,2,1024]{3,1,2,0:T(8,128)(2,1)S(1)} %stack.3), channel_id=1, replica_groups=mesh['section'=2,'dp'=16,'tensor'=4] {'tensor'}, dimensions={0} | all-to-all | bytes 8388608 | tf_op jit(solution)/shard_map/all_to_all | solution.py:19
  195.8 1.1 convert_bitcast_fusion
  196.8 1.7 copy.76
  198.5 0.9 fusion.2
  199.4 0.0 copy-start.8
  199.4 1.5 broadcast_divide_fusion
  200.9 3.2 copy-done
  204.1 8.2 %convolution_bitcast_fusion = f32[4096,1024]{1,0:T(8,128)} fusion(bf16[256,2,1024]{0,2,1:T(8,128)(2,1)S(1)} %bitcast.114, f32[256,2,4096]{2,0,1:T(8,128)S(1)} %broadcast_divide_fusion, f32[4096]{0:T(1024)S(1)} %bitcast.124), kind=kOutput, calls=%fused_computation.5 | convolution fusion | flops 4299161600 | bytes 26230784 | tf_op jit(solution)/shard_map/ibd,ibc->dc/dot_general | solution.py:167
  212.3 0.0 reduce-scatter.6.cloned.1.call-update
  212.4 0.6 copy-done.10
  213.0 2.2 reduce-scatter.4.cloned.1.call-done
  215.2 2.9 multiply_reduce_fusion
  218.1 6.5 %psum.14 = f32[256,2,1]{0,1,2:T(2,128)S(1)} all-reduce(f32[256,2,1]{0,1,2:T(2,128)S(1)} %bitcast.127), channel_id=1, replica_groups=mesh['section'=2,'dp'=16,'tensor'=4] {'tensor'}, use_global_device_ids=true, to_apply=%region_6.7 | all-reduce | flops 512 | bytes 4096 | tf_op jit(solution)/shard_map/psum | solution.py:116
  224.6 2.3 fusion.10
  226.9 0.6 gather_fusion
  227.6 0.2 select_bitcast_fusion
  227.7 5.1 %collective-permute-start = (bf16[256,2,1024]{2,0,1:T(8,128)(2,1)S(1)}, bf16[256,2,1024]{2,0,1:T(8,128)(2,1)S(1)}, u32[]{:S(2)}, u32[]{:S(2)}) collective-permute-start(bf16[256,2,1024]{2,0,1:T(8,128)(2,1)S(1)} %select_bitcast_fusion), channel_id=1, source_target_pairs={{64,0},{65,1},{66,2},{67,3},{68,4},{69,5},{70,6},{71,7},{72,8},{73... | collective-permute-start | bytes 3145736 | tf_op jit(solution)/shard_map/ppermute | solution.py:29
  232.8 33.7 %psum.15 = f32[1024]{0:T(1024)S(1)} all-reduce(f32[1024]{0:T(1024)S(1)} %get-tuple-element.12), channel_id=1, replica_groups=mesh['section'=2,'dp'=16,'tensor'=4] {'dp'}, use_global_device_ids=true, to_apply=%region_10.11 | all-reduce | flops 1024 | bytes 8192 | tf_op jit(solution)/shard_map/psum | solution.py:175
  266.5 0.6 broadcast_multiply_fusion
  267.1 35.6 %reduce-scatter.8.cloned.1.call-done = f32[512,256]{1,0:T(8,128)} async-done(((f32[512,4096]{1,0:T(8,128)}), f32[512,256]{1,0:T(8,128)}) %reduce-scatter.8.cloned.1.call-update) | async-done | bytes 524304 | tf_op jit(solution)/shard_map/reduce_scatter | solution.py:174
  302.7 1.9 multiply_bitcast_fusion.1
  304.6 0.0 collective-permute-done
  304.6 2.0 copy.52
  306.6 110.5 %reduce-scatter.6.cloned.1.call-done = f32[256,1024]{1,0:T(8,128)} async-done(((f32[4096,1024]{1,0:T(8,128)}), f32[256,1024]{1,0:T(8,128)}) %reduce-scatter.6.cloned.1.call-update) | async-done | bytes 1048592 | tf_op jit(solution)/shard_map/reduce_scatter | solution.py:173
  417.1 2.3 multiply_bitcast_fusion
  (17 shorter events, 0.1 us)
Async XLA Ops:
  7.2 2.7 copy-start.6
  7.2 3.0 copy-start.7
  7.2 54.5 %all-gather.3.cloned.1.call-start = ((), (), s32[]{:S(2)}) async-start(), calls=%async_computation.7 | async-start | bytes 5242880 | tf_op jit(solution)/shard_map/all_gather | solution.py:81
  9.7 1.0 copy-start.4
  9.7 1.6 copy-start.9
  9.8 205.4 %reduce-scatter.4.cloned.1.call-start = ((), (), s32[]{:S(2)}) async-start(), calls=%async_computation.4 | async-start | bytes 10485760 | tf_op jit(solution)/shard_map/reduce_scatter | solution.py:110
  11.3 2.6 copy-start.5
  67.8 1.6 copy-start.11
  89.1 213.6 %reduce-scatter.8.cloned.1.call-start = ((), (), s32[]{:S(2)}) async-start(), calls=%async_computation.6 | async-start | bytes 8912896 | tf_op jit(solution)/shard_map/reduce_scatter | solution.py:174
  89.1 2.8 copy-start.2
  97.5 1.5 copy-start.3
  97.5 319.6 %reduce-scatter.6.cloned.1.call-start = ((), (), s32[]{:S(2)}) async-start(), calls=%async_computation.5 | async-start | bytes 17825792 | tf_op jit(solution)/shard_map/reduce_scatter | solution.py:173
  199.4 4.7 %copy-start.8 = (f32[1,4096]{1,0:T(1,128)S(1)}, f32[1,4096]{1,0:T(1,128)}, u32[]{:S(2)}) copy-start(f32[1,4096]{1,0:T(1,128)} %param.11) | copy-start | bytes 49156
  200.9 3.2 copy-start
  212.3 0.7 copy-start.10
  215.2 9.4 %copy-start.1 = (f32[256,2,1024]{2,0,1:T(8,128)S(1)}, f32[256,2,1024]{2,0,1:T(8,128)}, u32[]{:S(2)}) copy-start(f32[256,2,1024]{2,0,1:T(8,128)} %reduce-scatter.4.cloned.1.call-done) | copy-start | bytes 6291460
  227.7 76.8 %collective-permute-start = (bf16[256,2,1024]{2,0,1:T(8,128)(2,1)S(1)}, bf16[256,2,1024]{2,0,1:T(8,128)(2,1)S(1)}, u32[]{:S(2)}, u32[]{:S(2)}) collective-permute-start(bf16[256,2,1024]{2,0,1:T(8,128)(2,1)S(1)} %select_bitcast_fusion), channel_id=1, source_target_pairs={{64,0},{65,1},{66,2},{67,3},{68,4},{69,5},{70,6},{71,7},{72,8},{73... | collective-permute-start | bytes 3145736 | tf_op jit(solution)/shard_map/ppermute | solution.py:29
Sparse Core Ops, SparseCore 0:
  10.2 51.4 all-gather.2
  89.2 125.9 reduce-scatter.3
  218.6 84.0 reduce-scatter.7
  306.0 111.1 reduce-scatter.5
